TPU v7x, 32 devices: a whole 2x2x4 slice. The times are simulated.
32 devices in a mesh: inp: 8 (over z, core), tm: 4 (over y, x).
Axes of the slice: x: 2, y: 2, z: 4, core: 2. Of those that a mesh axis runs over, the one named last changes fastest.
Arguments:
- samples: bfloat16 [256, 786432], P('inp', 'tm'), may hold values from -6 to 6
- tap_weights: float32 [4, 512], replicated, may hold values from -3 to 3
Outputs:
- visibilities: float32 [256, 2, 256, 256], P('tm', None, 'inp')
All inputs are finite; a program needn't handle non-finite values.
Results may differ from a plain program's by a relative error of at most 0.00081.
Values may be sent and summed in bfloat16 or wider, within the bound.
A program may use at most 128 MiB of HBM per device.

v0:
```python
import math

import jax
import jax.numpy as jnp
from jax import lax
from jax.sharding import PartitionSpec as P


def passed_along(block, axis, distance):
    devices = range(lax.axis_size(axis))
    route = [(i - distance, i) for i in devices if i - distance in devices]
    return lax.ppermute(block, axis, route)


def filter_taps(extended, weights, count):
    total = weights[0][None, None, :] * extended[:, 0:count, :].astype(jnp.float32)
    for tap in range(1, weights.shape[0]):
        total = total + weights[tap][None, None, :] * extended[:, tap : tap + count, :].astype(
            jnp.float32
        )
    return total


def per_device(samples, tap_weights):
    in_dev = samples.shape[0]
    frame = tap_weights.shape[1]
    taps = tap_weights.shape[0]
    rim = taps - 1
    spectra_dev = samples.shape[1] // frame
    frames = samples.reshape(in_dev, spectra_dev, frame)
    before = passed_along(frames[:, spectra_dev - rim :, :], "tm", 1)
    filtered = filter_taps(jnp.concatenate([before, frames], axis=1), tap_weights, spectra_dev)
    n_inp = lax.axis_size("inp")
    n_time = lax.axis_size("tm")
    ch_dev = frame // 2 // n_inp
    column = jnp.arange(frame, dtype=jnp.int32)
    remain = column % (2 * ch_dev)
    channel = column // (2 * ch_dev) * ch_dev + remain % ch_dev
    is_real = remain // ch_dev == 0
    index_n = jnp.arange(frame, dtype=jnp.int32)
    phase = index_n[:, None] * channel[None, :] % frame
    angle = phase.astype(jnp.float32) * (2.0 * math.pi / frame)
    table = jnp.where(is_real[None, :], jnp.cos(angle), -jnp.sin(angle)) * frame ** (-0.5)
    spectra = jnp.einsum(
        "isn,nj->ijs",
        filtered,
        table,
        precision=lax.Precision.HIGHEST,
        preferred_element_type=jnp.float32,
    ).astype(jnp.bfloat16)
    turned = lax.all_to_all(spectra, "inp", split_axis=1, concat_axis=0, tiled=True)
    inputs = turned.shape[0]
    turned = turned.reshape(inputs, 2, ch_dev, spectra_dev)
    real_part = jnp.einsum("ipcs,jpcs->icj", turned, turned, preferred_element_type=jnp.float32)
    imag_part = jnp.einsum(
        "ics,jcs->icj", turned[:, 1], turned[:, 0], preferred_element_type=jnp.float32
    ) - jnp.einsum("ics,jcs->icj", turned[:, 0], turned[:, 1], preferred_element_type=jnp.float32)
    mine = lax.psum_scatter(
        jnp.stack([real_part, imag_part], axis=1), "tm", scatter_dimension=0, tiled=True
    )
    return mine * (1.0 / math.sqrt(spectra_dev * n_time))


def solution(mesh):
    return jax.shard_map(
        per_device,
        mesh=mesh,
        in_specs=(P("inp", "tm"), P()),
        out_specs=P("tm", None, "inp", None),
        check_vma=False,
    )
```

profile of v0, /device:TPU:25, one launch (start us, length us, event | category | flops | bytes accessed | tf_op | source)
XLA Modules:
  0.0 653.1 jit_solution(13122239102143808897)
XLA Ops:
  6.5 0.0 reduce-scatter.2.cloned.1.call-start
  6.5 0.0 copy-start.1
  6.5 9.3 %copy.28 = bf16[4,8,384,512]{3,2,1,0:T(8,128)(2,1)S(1)} copy(bf16[4,8,384,512]{3,1,2,0:T(8,128)(2,1)} %bitcast.50) | data formatting | bytes 25165824
  15.9 0.1 slice.42
  16.0 3.1 collective-permute-start
  19.1 4.3 fusion.79
  23.5 0.0 copy-done.1
  23.5 0.0 collective-permute-done
  23.5 51.5 %convert_bitcast_fusion = bf16[32,512,384]{2,1,0:T(8,128)(2,1)S(1)} fusion(bf16[32,384,512]{2,1,0:T(8,128)(2,1)S(1)} %bitcast.49, bf16[32,3,512]{2,1,0:T(4,128)(2,1)S(1)} %collective-permute-done, f32[512]{0:T(512)S(1)} %bitcast.53, f32[512]{0:T(512)S(1)} %bitcast.54, f32[512]{0:T(512)S(1)} %bitcast.52, f32[512]{0:T(512)S(1)} %bitcast.51, ...), kind=kOutput, calls=%fused_computation.24 | convolution fusion | flops 38786826240 | bytes 26320896 | tf_op jit(solution)/shard_map/isn,nj->ijs/dot_general | solution.py:44
  75.0 32.5 %copy.16 = bf16[32,512,384]{2,0,1:T(8,128)(2,1)S(1)} copy(bf16[32,512,384]{2,1,0:T(8,128)(2,1)S(1)} %convert_bitcast_fusion) | data formatting | bytes 25165824 | tf_op jit(solution)/shard_map/convert_element_type | solution.py:50
  107.6 276.6 %all_to_all.15 = bf16[32,512,384]{2,0,1:T(8,128)(2,1)S(1)} all-to-all(bf16[32,512,384]{2,0,1:T(8,128)(2,1)S(1)} %copy.16), channel_id=1, replica_groups=mesh['inp'=8,'tm'=4] {'inp'}, dimensions={1} | all-to-all | bytes 25165824 | tf_op jit(solution)/shard_map/all_to_all | solution.py:51
  384.2 14.8 %copy.18 = bf16[8,32,64,384]{3,2,1,0:T(8,128)(2,1)S(1)} copy(bf16[8,32,64,384]{3,1,2,0:T(8,128)(2,1)S(1)} %bitcast.47) | data formatting | bytes 25165824 | tf_op jit(solution)/shard_map/all_to_all | solution.py:51
  399.0 0.0 copy-start
  399.0 4.4 copy-done
  403.4 6.4 fusion.71
  409.8 20.0 %fusion.30 = f32[256,1,32,256]{0,3,2,1:T(8,128)} fusion(bf16[256,2,32,384]{3,2,1,0:T(8,128)(2,1)} %bitcast.46), kind=kOutput, calls=%fused_computation.34 | convolution fusion | flops 3221225472 | bytes 20971520 | tf_op jit(solution)/shard_map/ipcs,jpcs->icj/dot_general | solution.py:54
  429.9 11.5 %fusion.28 = f32[32,256,256]{2,1,0:T(8,128)} fusion(bf16[256,1,32,384]{3,2,1,0:T(8,128)(2,1)} %get-tuple-element.6, bf16[256,1,32,384]{3,2,1,0:T(8,128)(2,1)} %get-tuple-element.5), kind=kOutput, calls=%fused_computation.32 | convolution fusion | flops 1610612736 | bytes 20971520 | tf_op jit(solution)/shard_map/ics,jcs->icj/dot_general | solution.py:57
  441.4 14.1 %subtract_bitcast_fusion = f32[256,1,32,256]{0,3,2,1:T(8,128)} fusion(f32[32,256,256]{2,1,0:T(8,128)} %fusion.28, bf16[256,1,32,384]{3,2,1,0:T(8,128)(2,1)} %get-tuple-element.5, bf16[256,1,32,384]{3,2,1,0:T(8,128)(2,1)} %get-tuple-element.6), kind=kOutput, calls=%fused_computation.29 | convolution fusion | flops 1612709888 | bytes 29360128 | tf_op jit(solution)/shard_map/ics,jcs->icj/dot_general | solution.py:55
  455.5 11.5 %pad_maximum_fusion = f32[256,2,32,256]{0,3,2,1:T(8,128)} fusion(f32[256,1,32,256]{0,3,2,1:T(8,128)} %subtract_bitcast_fusion, f32[256,1,32,256]{0,3,2,1:T(8,128)} %fusion.30), kind=kLoop, calls=%fused_computation.14 | loop fusion | flops 4194304 | bytes 33554432 | tf_op jit(solution)/shard_map/stack | solution.py:59
  467.0 19.9 %copy.23 = f32[256,2,32,256]{3,2,1,0:T(8,128)} copy(f32[256,2,32,256]{0,3,2,1:T(8,128)} %pad_maximum_fusion) | data formatting | bytes 33554432 | tf_op jit(solution)/shard_map/stack | solution.py:59
  486.9 0.0 reduce-scatter.2.cloned.1.call-update
  487.0 153.8 %reduce-scatter.2.cloned.1.call-done = f32[64,2,32,256]{3,2,1,0:T(8,128)} async-done(((f32[256,2,32,256]{3,2,1,0:T(8,128)}), f32[64,2,32,256]{3,2,1,0:T(8,128)}) %reduce-scatter.2.cloned.1.call-update) | async-done | bytes 4194320 | tf_op jit(solution)/shard_map/reduce_scatter | solution.py:58
  640.7 5.1 broadcast_multiply_fusion
  (3 shorter events, 0.0 us)
Async XLA Ops:
  6.5 634.2 %reduce-scatter.2.cloned.1.call-start = ((), (), s32[]{:S(2)}) async-start(), calls=%async_computation.2 | async-start | bytes 20971520 | tf_op jit(solution)/shard_map/reduce_scatter | solution.py:58
  6.5 16.9 %copy-start.1 = (f32[4,512]{1,0:T(4,128)S(1)}, f32[4,512]{1,0:T(4,128)}, u32[]{:S(2)}) copy-start(f32[4,512]{1,0:T(4,128)} %param.3) | copy-start | bytes 24580
  16.0 7.5 %collective-permute-start = (bf16[32,3,512]{2,1,0:T(4,128)(2,1)S(1)}, bf16[32,3,512]{2,1,0:T(4,128)(2,1)S(1)}, u32[]{:S(2)}, u32[]{:S(2)}) collective-permute-start(bf16[32,3,512]{2,1,0:T(4,128)(2,1)S(1)} %slice.42), channel_id=1, source_target_pairs={{0,1},{1,2},{2,3},{4,5},{5,6},{6,7},{8,9},{9,10},{10,11},{12,13},{... | collective-permute-start | bytes 294920 | tf_op jit(solution)/shard_map/ppermute | solution.py:12
  399.0 4.5 copy-start
Sparse Core Ops, SparseCore 0:
  487.1 153.5 reduce-scatter.1
where the time goes:
time: 661 us; the launch traced here: 653 us
  blocking collectives  277 us (42%)
  waiting for transfers between devices  154 us (23%)
  matrix products  97.2 us (15%)
  local copies, waits for them, and re-layouts  87.5 us (13%)
  other arithmetic  21 us (3%)
  between operations  13.9 us (2%)
    all_to_all x1, blocking collectives, per_device(): lax.all_to_all(spectra, 'inp', split_axis=1, concat_axis=0, tiled=True)  277 us
    reduce_scatter x1, waiting for transfers between devices, per_device(): lax.psum_scatter(jnp.stack([real_part, imag_part], axis=1), 'tm', scatter...  154 us
    dot_general x1, matrix products, per_device(): jnp.einsum('isn,nj->ijs', filtered, table, precision=lax.Precision.HIGHES...  51.5 us
    convert_element_type x1, local copies, waits for them, and re-layouts, per_device(): spectra = jnp.einsum('isn,nj->ijs', filtered, table, precision=lax.Precis...  32.5 us
    dot_general x1, matrix products, per_device(): jnp.einsum('ipcs,jpcs->icj', turned, turned, preferred_element_type=jnp.f...  20 us
    another operation x1, local copies, waits for them, and re-layouts, per_device(): jnp.stack([real_part, imag_part], axis=1)  19.9 us
    all_to_all x1, local copies, waits for them, and re-layouts, per_device(): lax.all_to_all(spectra, 'inp', split_axis=1, concat_axis=0, tiled=True)  14.8 us
    dot_general x1, matrix products, per_device(): jnp.einsum('ics,jcs->icj', turned[:, 1], turned[:, 0], preferred_element_...  14.1 us
  transfers between devices with their start and end apart: 2, of which 1 were waited for; matrix products, arithmetic and copies ran while one was open for 1% of the time, Pallas kernels for 0%

commit v1 on v0

v1 whole, which is shorter than its diff:
```python
import functools
import math

import jax
import jax.numpy as jnp
from jax import lax
from jax.experimental import pallas as pl
from jax.experimental.pallas import tpu as pltpu
from jax.sharding import PartitionSpec as P

MESH = pl.DeviceIdType.MESH
STEPS = 8
AHEAD = 2


def passed_along(block, axis, distance):
    devices = range(lax.axis_size(axis))
    route = [(i - distance, i) for i in devices if i - distance in devices]
    return lax.ppermute(block, axis, route)


def filter_taps(extended, weights, count):
    total = weights[0][None, None, :] * extended[:, 0:count, :].astype(jnp.float32)
    for tap in range(1, weights.shape[0]):
        total = total + weights[tap][None, None, :] * extended[:, tap : tap + count, :].astype(
            jnp.float32
        )
    return total


def exchange_and_correlate(
    n_inp, n_tm, steps, scale, spec, out, recv, part, got, send_sem, recv_sem, own_sem, put_sem, got_sem
):
    me = lax.axis_index("inp")
    seg = lax.axis_index("tm")
    ch_dev, _, in_dev, width = recv.shape
    per = ch_dev // steps
    inputs = n_inp * in_dev
    rows = inputs // n_tm
    half = width // 2

    barrier = pltpu.get_barrier_semaphore()
    for d in range(1, n_inp):
        pl.semaphore_signal(
            barrier, inc=1, device_id={"inp": lax.rem(me + d, n_inp)}, device_id_type=MESH
        )
    for d in range(1, n_tm):
        pl.semaphore_signal(
            barrier, inc=1, device_id={"tm": lax.rem(seg + d, n_tm)}, device_id_type=MESH
        )
    pl.semaphore_wait(barrier, n_inp - 1 + n_tm - 1)

    def own_copy(g):
        chunk = pl.ds(g * per, per)
        return pltpu.make_async_copy(spec.at[me, chunk], recv.at[chunk, me], own_sem.at[g])

    def turn_copy(g, d):
        chunk = pl.ds(g * per, per)
        peer = lax.rem(me + d, n_inp)
        return pltpu.make_async_remote_copy(
            src_ref=spec.at[peer, chunk],
            dst_ref=recv.at[chunk, me],
            send_sem=send_sem.at[g, d - 1],
            recv_sem=recv_sem.at[g, d - 1],
            device_id={"inp": peer},
            device_id_type=MESH,
        )

    def sum_copy(g, d):
        chunk = pl.ds(g * per, per)
        peer = lax.rem(seg + d, n_tm)
        return pltpu.make_async_remote_copy(
            src_ref=part.at[peer, chunk],
            dst_ref=got.at[d - 1, chunk],
            send_sem=put_sem.at[g, d - 1],
            recv_sem=got_sem.at[g, d - 1],
            device_id={"tm": peer},
            device_id_type=MESH,
        )

    def each(first, end, body):
        def step(d, carry):
            body(d)
            return carry

        lax.fori_loop(first, end, step, 0)

    def send(g):
        own_copy(g).start()
        each(1, n_inp, lambda d: turn_copy(g, d).start())

    def correlate(ch):
        block = recv[ch]
        if in_dev % 16 == 0:
            x = block.reshape(inputs, width)
        else:
            x = block.astype(jnp.float32).reshape(inputs, width).astype(jnp.bfloat16)
        y = jnp.concatenate([x[:, half:], -x[:, :half]], axis=1)
        for p, left in ((0, x), (1, y)):
            product = lax.dot_general(
                left, x, (((1,), (1,)), ((), ())), preferred_element_type=jnp.float32
            )
            for q in range(n_tm):
                part[q, ch, p] = product[q * rows : (q + 1) * rows]

    def finish(g):
        each(1, n_tm, lambda d: sum_copy(g, d).wait_recv())

        def add(k):
            ch = g * per + k
            total = part[seg, ch]
            for d in range(1, n_tm):
                total = total + got[d - 1, ch]
            out[ch] = total * scale

        each(0, per, add)

    for g in range(min(AHEAD, steps)):
        send(g)

    def step(g):
        @pl.when(g + AHEAD < steps)
        def _():
            send(g + AHEAD)

        own_copy(g).wait()
        each(1, n_inp, lambda d: turn_copy(g, d).wait_recv())
        each(0, per, lambda k: correlate(g * per + k))
        each(1, n_tm, lambda d: sum_copy(g, d).start())

        @pl.when(g >= 1)
        def _():
            finish(g - 1)

    each(0, steps, step)
    finish(steps - 1)

    def drain(g):
        each(1, n_inp, lambda d: turn_copy(g, d).wait_send())
        each(1, n_tm, lambda d: sum_copy(g, d).wait_send())

    each(0, steps, drain)


def per_device(samples, tap_weights):
    in_dev = samples.shape[0]
    frame = tap_weights.shape[1]
    taps = tap_weights.shape[0]
    rim = taps - 1
    spectra_dev = samples.shape[1] // frame
    frames = samples.reshape(in_dev, spectra_dev, frame)
    before = passed_along(frames[:, spectra_dev - rim :, :], "tm", 1)
    filtered = filter_taps(jnp.concatenate([before, frames], axis=1), tap_weights, spectra_dev)
    n_inp = lax.axis_size("inp")
    n_tm = lax.axis_size("tm")
    ch_dev = frame // 2 // n_inp
    column = jnp.arange(frame, dtype=jnp.int32)
    channel = column // 2
    is_real = column % 2 == 0
    index_n = jnp.arange(frame, dtype=jnp.int32)
    phase = index_n[:, None] * channel[None, :] % frame
    angle = phase.astype(jnp.float32) * (2.0 * math.pi / frame)
    table = jnp.where(is_real[None, :], jnp.cos(angle), -jnp.sin(angle)) * frame ** (-0.5)
    spectra = jnp.einsum(
        "isn,nj->ijs",
        filtered,
        table,
        precision=lax.Precision.HIGH,
        preferred_element_type=jnp.float32,
    ).astype(jnp.bfloat16)
    spectra = spectra.reshape(in_dev, n_inp, ch_dev, 2 * spectra_dev).transpose(1, 2, 0, 3)
    steps = math.gcd(STEPS, ch_dev)
    inputs = n_inp * in_dev
    rows = inputs // n_tm
    scale = 1.0 / math.sqrt(spectra_dev * n_tm)
    mine = pl.pallas_call(
        functools.partial(exchange_and_correlate, n_inp, n_tm, steps, scale),
        out_shape=jax.ShapeDtypeStruct((ch_dev, 2, rows, inputs), jnp.float32),
        in_specs=[pl.BlockSpec(memory_space=pltpu.HBM)],
        out_specs=pl.BlockSpec(memory_space=pltpu.VMEM),
        scratch_shapes=[
            pltpu.VMEM((ch_dev, n_inp, in_dev, 2 * spectra_dev), jnp.bfloat16),
            pltpu.VMEM((n_tm, ch_dev, 2, rows, inputs), jnp.float32),
            pltpu.VMEM((n_tm - 1, ch_dev, 2, rows, inputs), jnp.float32),
            pltpu.SemaphoreType.DMA((steps, n_inp - 1)),
            pltpu.SemaphoreType.DMA((steps, n_inp - 1)),
            pltpu.SemaphoreType.DMA((steps,)),
            pltpu.SemaphoreType.DMA((steps, n_tm - 1)),
            pltpu.SemaphoreType.DMA((steps, n_tm - 1)),
        ],
        compiler_params=pltpu.CompilerParams(
            collective_id=0, has_side_effects=True, vmem_limit_bytes=60 << 20
        ),
    )(spectra)
    return mine.transpose(2, 1, 0, 3)


def solution(mesh):
    return jax.shard_map(
        per_device,
        mesh=mesh,
        in_specs=(P("inp", "tm"), P()),
        out_specs=P("tm", None, "inp", None),
        check_vma=False,
    )
```

time: 661 us -> 424 us (0.64); the launches traced: 653 us -> 423 us
  Pallas kernels: 0 us -> 319 us
  blocking collectives: 277 us -> 0 us
  waiting for transfers between devices: 154 us -> 0.01 us
  matrix products: 97.2 us -> 42.6 us
  local copies, waits for them, and re-layouts: 87.5 us -> 53.7 us
  other arithmetic: 21 us -> 4.33 us
  between operations: 13.9 us -> 0.08 us
    pallas_call x0 -> x1, Pallas kernels: none -> 319 us  [per_device(): pl.pallas_call(functools.partial(exchange_and_correlate, n_inp, n_tm, ste...]
    all_to_all x1 -> x0, blocking collectives: 277 us -> none  [per_device(): lax.all_to_all(spectra, 'inp', split_axis=1, concat_axis=0, tiled=True)]
    reduce_scatter x1 -> x0, waiting for transfers between devices: 154 us -> none  [per_device(): lax.psum_scatter(jnp.stack([real_part, imag_part], axis=1), 'tm', scatter...]
    dot_general x4 -> x1, matrix products: 97.2 us -> 42.6 us  [per_device(): jnp.einsum('isn,nj->ijs', filtered, table, precision=lax.Precision.HIGH,...]
    reshape x0 -> x2, local copies, waits for them, and re-layouts: none -> 33.1 us  [per_device(): spectra.reshape(in_dev, n_inp, ch_dev, 2 * spectra_dev)]
    convert_element_type x1 -> x0, local copies, waits for them, and re-layouts: 32.5 us -> none  [per_device(): spectra = jnp.einsum('isn,nj->ijs', filtered, table, precision=lax.Precis...]
    another operation x1 -> x0, local copies, waits for them, and re-layouts: 19.9 us -> none  [per_device(): jnp.stack([real_part, imag_part], axis=1)]
    all_to_all x1 -> x0, local copies, waits for them, and re-layouts: 14.8 us -> none  [per_device(): lax.all_to_all(spectra, 'inp', split_axis=1, concat_axis=0, tiled=True)]
  transfers between devices with their start and end apart: 2 -> 1, of which waited for: 1 -> 0; matrix products, arithmetic and copies ran while one was open for 1% -> 1% of each run, Pallas kernels for 0% -> 0%
where the time goes in v1:
time: 424 us; the launch traced here: 423 us
  Pallas kernels  319 us (75%)
  local copies, waits for them, and re-layouts  53.7 us (13%)
  matrix products  42.6 us (10%)
  other arithmetic  4.33 us (1%)
    pallas_call x1, Pallas kernels, per_device(): pl.pallas_call(functools.partial(exchange_and_correlate, n_inp, n_tm, ste...  319 us
    dot_general x1, matrix products, per_device(): jnp.einsum('isn,nj->ijs', filtered, table, precision=lax.Precision.HIGH,...  42.6 us
    reshape x2, local copies, waits for them, and re-layouts, per_device(): spectra.reshape(in_dev, n_inp, ch_dev, 2 * spectra_dev)  33.1 us
    unnamed x5, local copies, waits for them, and re-layouts  13.8 us
  transfers between devices with their start and end apart: 1, of which 0 were waited for; matrix products, arithmetic and copies ran while one was open for 1% of the time, Pallas kernels for 0%

profile of v1, /device:TPU:25, one launch (start us, length us, event | category | flops | bytes accessed | tf_op | source)
XLA Modules:
  0.0 422.7 jit_solution(6113470525144318196)
XLA Ops:
  0.0 0.0 copy-start.1
  0.0 9.3 %copy.6 = bf16[4,8,384,512]{3,2,1,0:T(8,128)(2,1)S(1)} copy(bf16[4,8,384,512]{3,1,2,0:T(8,128)(2,1)} %bitcast.26) | data formatting | bytes 25165824
  9.3 0.0 copy-start
  9.4 4.5 %copy-done = bf16[4,8,384,512]{3,2,1,0:T(8,128)(2,1)} copy-done((bf16[4,8,384,512]{3,2,1,0:T(8,128)(2,1)}, bf16[4,8,384,512]{3,2,1,0:T(8,128)(2,1)S(1)}, u32[]{:S(2)}) %copy-start) | copy-done | bytes 12582936
  13.8 0.1 slice.32
  13.9 3.1 collective-permute-start
  17.0 4.3 %fusion.67 = f32[512,512,1]{0,1,2:T(8,128)S(1)} fusion(s32[512]{0:T(512)S(1)} %add_select_fusion.1, pred[512]{0:T(512)(128)(4,1)S(1)} %fusion.48), kind=kLoop, calls=%fused_computation.33.clone.2 | loop fusion | flops 4456448 | bytes 1051136 | tf_op jit(solution)/shard_map/isn,nj->ijs/dot_general | solution.py:164
  21.4 0.0 copy-done.1
  21.4 0.0 collective-permute-done
  21.4 42.6 %convert_bitcast_fusion = bf16[32,512,384]{2,1,0:T(8,128)(2,1)} fusion(bf16[32,384,512]{2,1,0:T(8,128)(2,1)} %bitcast.25, bf16[32,3,512]{2,1,0:T(4,128)(2,1)S(1)} %collective-permute-done, f32[512]{0:T(512)S(1)} %bitcast.29, f32[512]{0:T(512)S(1)} %bitcast.30, f32[512]{0:T(512)S(1)} %bitcast.28, f32[512]{0:T(512)S(1)} %bitcast.27, ...), kind=kOutput, calls=%fused_computation.22 | convolution fusion | flops 19459473408 | bytes 26320896 | tf_op jit(solution)/shard_map/isn,nj->ijs/dot_general | solution.py:164
  64.0 18.9 %reshape.34 = bf16[32,8,32,768]{3,2,1,0:T(8,128)(2,1)} reshape(bf16[32,512,384]{2,1,0:T(8,128)(2,1)} %convert_bitcast_fusion) | data formatting | bytes 25165824 | tf_op jit(solution)/shard_map/reshape | solution.py:171
  82.9 14.2 %copy.8 = bf16[32,8,32,768]{3,0,2,1:T(8,128)(2,1)} copy(bf16[32,8,32,768]{3,2,1,0:T(8,128)(2,1)} %reshape.34) | data formatting | bytes 25165824 | tf_op jit(solution)/shard_map/reshape | solution.py:171
  97.1 319.0 %shard_map.28 = f32[32,2,64,256]{3,2,1,0:T(8,128)} custom-call(bf16[8,32,32,768]{3,2,1,0:T(8,128)(2,1)} %bitcast.22), custom_call_target="tpu_custom_call" | custom-call | tf_op jit(solution)/shard_map/pallas_call | solution.py:176
  416.1 6.6 %copy.5 = f32[64,2,32,256]{3,2,1,0:T(8,128)} copy(f32[64,2,32,256]{3,0,1,2:T(8,128)} %bitcast.23) | data formatting | bytes 8388608 | tf_op jit(solution)/shard_map/transpose | solution.py:195
  (3 shorter events, 0.0 us)
Async XLA Ops:
  0.0 21.4 %copy-start.1 = (f32[4,512]{1,0:T(4,128)S(1)}, f32[4,512]{1,0:T(4,128)}, u32[]{:S(2)}) copy-start(f32[4,512]{1,0:T(4,128)} %param.3) | copy-start | bytes 24580
  9.3 4.5 %copy-start = (bf16[4,8,384,512]{3,2,1,0:T(8,128)(2,1)}, bf16[4,8,384,512]{3,2,1,0:T(8,128)(2,1)S(1)}, u32[]{:S(2)}) copy-start(bf16[4,8,384,512]{3,2,1,0:T(8,128)(2,1)S(1)} %copy.6) | copy-start | bytes 37748740
  13.9 7.5 %collective-permute-start = (bf16[32,3,512]{2,1,0:T(4,128)(2,1)S(1)}, bf16[32,3,512]{2,1,0:T(4,128)(2,1)S(1)}, u32[]{:S(2)}, u32[]{:S(2)}) collective-permute-start(bf16[32,3,512]{2,1,0:T(4,128)(2,1)S(1)} %slice.32), channel_id=1, source_target_pairs={{0,1},{1,2},{2,3},{4,5},{5,6},{6,7},{8,9},{9,10},{10,11},{12,13},{... | collective-permute-start | bytes 294920 | tf_op jit(solution)/shard_map/ppermute | solution.py:19

commit v2 on v1

--- a/solution.py
+++ b/solution.py
@@ -3,14 +3,15 @@
 
 import jax
 import jax.numpy as jnp
+import numpy as np
 from jax import lax
 from jax.experimental import pallas as pl
 from jax.experimental.pallas import tpu as pltpu
 from jax.sharding import PartitionSpec as P
 
 MESH = pl.DeviceIdType.MESH
-STEPS = 8
-AHEAD = 2
+STEPS = 16
+AHEAD = 4
 
 
 def passed_along(block, axis, distance):
@@ -29,15 +30,16 @@
 
 
 def exchange_and_correlate(
-    n_inp, n_tm, steps, scale, spec, out, recv, part, got, send_sem, recv_sem, own_sem, put_sem, got_sem
+    n_inp, n_tm, steps, scale, even, odd, out, recv, part, got, send_sem, recv_sem, own_sem, put_sem, got_sem
 ):
     me = lax.axis_index("inp")
     seg = lax.axis_index("tm")
-    ch_dev, _, in_dev, width = recv.shape
+    ch_dev, _, _, in_dev, count = recv.shape
     per = ch_dev // steps
     inputs = n_inp * in_dev
     rows = inputs // n_tm
-    half = width // 2
+    fold = ch_dev // 2
+    turn = steps // 2
 
     barrier = pltpu.get_barrier_semaphore()
     for d in range(1, n_inp):
@@ -50,16 +52,16 @@
         )
     pl.semaphore_wait(barrier, n_inp - 1 + n_tm - 1)
 
-    def own_copy(g):
-        chunk = pl.ds(g * per, per)
-        return pltpu.make_async_copy(spec.at[me, chunk], recv.at[chunk, me], own_sem.at[g])
-
-    def turn_copy(g, d):
-        chunk = pl.ds(g * per, per)
+    def own_copy(g, spec=even, at=0):
+        return pltpu.make_async_copy(
+            spec.at[me, pl.ds(at * per, per)], recv.at[pl.ds(g * per, per), :, me], own_sem.at[g]
+        )
+
+    def turn_copy(g, d, spec=even, at=0):
         peer = lax.rem(me + d, n_inp)
         return pltpu.make_async_remote_copy(
-            src_ref=spec.at[peer, chunk],
-            dst_ref=recv.at[chunk, me],
+            src_ref=spec.at[peer, pl.ds(at * per, per)],
+            dst_ref=recv.at[pl.ds(g * per, per), :, me],
             send_sem=send_sem.at[g, d - 1],
             recv_sem=recv_sem.at[g, d - 1],
             device_id={"inp": peer},
@@ -85,17 +87,30 @@
 
         lax.fori_loop(first, end, step, 0)
 
+    def send_from(g, spec, at):
+        own_copy(g, spec, at).start()
+        each(1, n_inp, lambda d: turn_copy(g, d, spec, at).start())
+
     def send(g):
-        own_copy(g).start()
-        each(1, n_inp, lambda d: turn_copy(g, d).start())
+        @pl.when(g < turn)
+        def _():
+            send_from(g, even, g)
+
+        @pl.when(g >= turn)
+        def _():
+            send_from(g, odd, g - turn)
+
+    def side(ch, p):
+        block = recv[ch, p]
+        if in_dev % 16 == 0:
+            return block.reshape(inputs, count)
+        return block.astype(jnp.float32).reshape(inputs, count).astype(jnp.bfloat16)
 
     def correlate(ch):
-        block = recv[ch]
-        if in_dev % 16 == 0:
-            x = block.reshape(inputs, width)
-        else:
-            x = block.astype(jnp.float32).reshape(inputs, width).astype(jnp.bfloat16)
-        y = jnp.concatenate([x[:, half:], -x[:, :half]], axis=1)
+        real = side(ch, 0)
+        imag = side(ch, 1)
+        x = jnp.concatenate([real, imag], axis=1)
+        y = jnp.concatenate([imag, -real], axis=1)
         for p, left in ((0, x), (1, y)):
             product = lax.dot_general(
                 left, x, (((1,), (1,)), ((), ())), preferred_element_type=jnp.float32
@@ -111,7 +126,7 @@
             total = part[seg, ch]
             for d in range(1, n_tm):
                 total = total + got[d - 1, ch]
-            out[ch] = total * scale
+            out[lax.rem(ch, fold) * 2 + ch // fold] = total * scale
 
         each(0, per, add)
 
@@ -154,21 +169,24 @@
     n_inp = lax.axis_size("inp")
     n_tm = lax.axis_size("tm")
     ch_dev = frame // 2 // n_inp
-    column = jnp.arange(frame, dtype=jnp.int32)
-    channel = column // 2
-    is_real = column % 2 == 0
-    index_n = jnp.arange(frame, dtype=jnp.int32)
-    phase = index_n[:, None] * channel[None, :] % frame
-    angle = phase.astype(jnp.float32) * (2.0 * math.pi / frame)
-    table = jnp.where(is_real[None, :], jnp.cos(angle), -jnp.sin(angle)) * frame ** (-0.5)
-    spectra = jnp.einsum(
-        "isn,nj->ijs",
-        filtered,
-        table,
-        precision=lax.Precision.HIGH,
-        preferred_element_type=jnp.float32,
-    ).astype(jnp.bfloat16)
-    spectra = spectra.reshape(in_dev, n_inp, ch_dev, 2 * spectra_dev).transpose(1, 2, 0, 3)
+    fold = frame // 2
+    low, high = filtered[:, :, :fold], filtered[:, :, fold:]
+    sides = []
+    for odd, folded in ((0, low + high), (1, low - high)):
+        column = np.arange(fold)
+        channel = column // 2 * 2 + odd
+        phase = np.arange(fold)[:, None] * channel[None, :] % frame
+        angle = phase * (2.0 * math.pi / frame)
+        table = np.where(column % 2 == 0, np.cos(angle), -np.sin(angle)) * frame ** (-0.5)
+        side = jnp.einsum(
+            "isn,nj->ijs",
+            folded,
+            jnp.asarray(table, jnp.float32),
+            precision=lax.Precision.HIGH,
+            preferred_element_type=jnp.float32,
+        ).astype(jnp.bfloat16)
+        side = side.reshape(in_dev, n_inp, ch_dev // 2, 2, spectra_dev)
+        sides.append(side.transpose(1, 2, 3, 0, 4))
     steps = math.gcd(STEPS, ch_dev)
     inputs = n_inp * in_dev
     rows = inputs // n_tm
@@ -176,10 +194,10 @@
     mine = pl.pallas_call(
         functools.partial(exchange_and_correlate, n_inp, n_tm, steps, scale),
         out_shape=jax.ShapeDtypeStruct((ch_dev, 2, rows, inputs), jnp.float32),
-        in_specs=[pl.BlockSpec(memory_space=pltpu.HBM)],
+        in_specs=[pl.BlockSpec(memory_space=pltpu.HBM)] * 2,
         out_specs=pl.BlockSpec(memory_space=pltpu.VMEM),
         scratch_shapes=[
-            pltpu.VMEM((ch_dev, n_inp, in_dev, 2 * spectra_dev), jnp.bfloat16),
+            pltpu.VMEM((ch_dev, 2, n_inp, in_dev, spectra_dev), jnp.bfloat16),
             pltpu.VMEM((n_tm, ch_dev, 2, rows, inputs), jnp.float32),
             pltpu.VMEM((n_tm - 1, ch_dev, 2, rows, inputs), jnp.float32),
             pltpu.SemaphoreType.DMA((steps, n_inp - 1)),
@@ -191,7 +209,7 @@
         compiler_params=pltpu.CompilerParams(
             collective_id=0, has_side_effects=True, vmem_limit_bytes=60 << 20
         ),
-    )(spectra)
+    )(*sides)
     return mine.transpose(2, 1, 0, 3)
 
 

time: 424 us -> 393 us (0.927)
  local copies, waits for them, and re-layouts: 53.7 us -> 31.6 us
  matrix products: 42.6 us -> 23.6 us
  other arithmetic: 4.33 us -> 15 us
    reshape x2 -> x0, local copies, waits for them, and re-layouts: 33.1 us -> none  [per_device(): spectra.reshape(in_dev, n_inp, ch_dev, 2 * spectra_dev)]
    dot_general x1 -> x2, matrix products: 42.6 us -> 23.6 us  [per_device(): jnp.einsum('isn,nj->ijs', folded, jnp.asarray(table, jnp.float32), precis...]
    convert_element_type x0 -> x2, local copies, waits for them, and re-layouts: none -> 15.6 us  [per_device(): side = jnp.einsum('isn,nj->ijs', folded, jnp.asarray(table, jnp.float32),...]
    add x0 -> x1, other arithmetic: none -> 15 us  [filter_taps(): total + weights[tap][None, None, :] * extended[:, tap:tap + count, :].ast...]
    unnamed x5 -> x7, local copies, waits for them, and re-layouts: 13.8 us -> 9.35 us
    dot_general x1 -> x0, other arithmetic: 4.32 us -> none  [per_device(): jnp.einsum('isn,nj->ijs', filtered, table, precision=lax.Precision.HIGH,...]
  transfers between devices with their start and end apart: 1 -> 1, of which waited for: 0 -> 1; matrix products, arithmetic and copies ran while one was open for 1% -> 0% of each run, Pallas kernels for 0% -> 0%
where the time goes in v2:
time: 393 us; the launch traced here: 392 us
  Pallas kernels  317 us (81%)
  local copies, waits for them, and re-layouts  31.6 us (8%)
  matrix products  23.6 us (6%)
  other arithmetic  15 us (4%)
    pallas_call x1, Pallas kernels, per_device(): pl.pallas_call(functools.partial(exchange_and_correlate, n_inp, n_tm, ste...  317 us
    dot_general x2, matrix products, per_device(): jnp.einsum('isn,nj->ijs', folded, jnp.asarray(table, jnp.float32), precis...  23.6 us
    convert_element_type x2, local copies, waits for them, and re-layouts, per_device(): side = jnp.einsum('isn,nj->ijs', folded, jnp.asarray(table, jnp.float32),...  15.6 us
    add x1, other arithmetic, filter_taps(): total + weights[tap][None, None, :] * extended[:, tap:tap + count, :].ast...  15 us
    unnamed x7, local copies, waits for them, and re-layouts  9.35 us
  transfers between devices with their start and end apart: 1, of which 1 were waited for; matrix products, arithmetic and copies ran while one was open for 0% of the time, Pallas kernels for 0%

profile of v2, /device:TPU:25, one launch (start us, length us, event | category | flops | bytes accessed | tf_op | source)
XLA Modules:
  0.0 392.1 jit_solution(9809266960728317402)
XLA Ops:
  0.0 0.0 copy-start.2
  0.0 9.3 %copy.8 = bf16[4,8,384,512]{3,2,1,0:T(8,128)(2,1)S(1)} copy(bf16[4,8,384,512]{3,1,2,0:T(8,128)(2,1)} %bitcast.26) | data formatting | bytes 25165824
  9.3 0.0 copy-start
  9.4 0.1 slice.40
  9.4 3.1 collective-permute-start
  12.6 0.0 copy-done.2
  12.6 2.1 collective-permute-done
  14.7 0.0 copy-start.1
  14.7 15.0 %multiply_add_fusion = f32[32,384,512]{2,1,0:T(8,128)} fusion(bf16[32,384,512]{2,1,0:T(8,128)(2,1)S(1)} %bitcast.22, bf16[32,3,512]{2,1,0:T(4,128)(2,1)S(1)} %collective-permute-done, f32[512]{0:T(512)S(1)} %bitcast.29, f32[512]{0:T(512)S(1)} %bitcast.30, f32[512]{0:T(512)S(1)} %bitcast.28, f32[512]{0:T(512)S(1)} %bitcast.27), kind=kLoop, calls=%fused_computation | loop fusion | flops 125829120 | bytes 37855232 | tf_op jit(solution)/shard_map/add | solution.py:26
  29.7 0.0 copy-done
  29.7 10.9 %convert_bitcast_fusion.1 = bf16[32,256,384]{2,1,0:T(8,128)(2,1)S(1)} fusion(f32[256,256,1]{0,1,2:T(8,128)S(1)} %copy-done, f32[32,384,512]{2,1,0:T(8,128)} %multiply_add_fusion), kind=kOutput, calls=%fused_computation.15 | convolution fusion | flops 4838129664 | bytes 31719424 | tf_op jit(solution)/shard_map/isn,nj->ijs/dot_general | solution.py:181
  40.6 0.0 copy-done.1
  40.7 12.7 %convert_bitcast_fusion = bf16[32,256,384]{2,1,0:T(8,128)(2,1)} fusion(f32[256,256,1]{0,1,2:T(8,128)S(1)} %copy-done.1, f32[32,384,512]{2,1,0:T(8,128)} %multiply_add_fusion), kind=kOutput, calls=%fused_computation.14 | convolution fusion | flops 4838129664 | bytes 31719424 | tf_op jit(solution)/shard_map/isn,nj->ijs/dot_general | solution.py:181
  53.3 9.1 %copy.6 = bf16[32,256,384]{2,0,1:T(8,128)(2,1)} copy(bf16[32,256,384]{2,1,0:T(8,128)(2,1)} %convert_bitcast_fusion) | data formatting | bytes 12582912 | tf_op jit(solution)/shard_map/convert_element_type | solution.py:187
  62.5 6.4 %copy.5 = bf16[32,256,384]{2,0,1:T(8,128)(2,1)} copy(bf16[32,256,384]{2,1,0:T(8,128)(2,1)S(1)} %convert_bitcast_fusion.1) | data formatting | bytes 12582912 | tf_op jit(solution)/shard_map/convert_element_type | solution.py:187
  68.9 316.5 %shard_map.46 = f32[32,2,64,256]{3,2,1,0:T(8,128)} custom-call(bf16[8,16,2,32,384]{4,3,2,1,0:T(8,128)(2,1)} %bitcast.24, bf16[8,16,2,32,384]{4,3,2,1,0:T(8,128)(2,1)} %bitcast.23), custom_call_target="tpu_custom_call" | custom-call | tf_op jit(solution)/shard_map/pallas_call | solution.py:194
  385.5 6.6 %copy.7 = f32[64,2,32,256]{3,2,1,0:T(8,128)} copy(f32[64,2,32,256]{3,0,1,2:T(8,128)} %bitcast.25) | data formatting | bytes 8388608 | tf_op jit(solution)/shard_map/transpose | solution.py:213
  (1 shorter events, 0.0 us)
Async XLA Ops:
  0.0 12.6 %copy-start.2 = (f32[4,512]{1,0:T(4,128)S(1)}, f32[4,512]{1,0:T(4,128)}, u32[]{:S(2)}) copy-start(f32[4,512]{1,0:T(4,128)} %param.5) | copy-start | bytes 24580
  9.3 20.4 %copy-start = (f32[256,256,1]{0,1,2:T(8,128)S(1)}, f32[256,256,1]{0,1,2:T(8,128)}, u32[]{:S(2)}) copy-start(f32[256,256,1]{0,1,2:T(8,128)} %constant.6) | copy-start | bytes 786436
  9.4 5.3 %collective-permute-start = (bf16[32,3,512]{2,1,0:T(4,128)(2,1)S(1)}, bf16[32,3,512]{2,1,0:T(4,128)(2,1)S(1)}, u32[]{:S(2)}, u32[]{:S(2)}) collective-permute-start(bf16[32,3,512]{2,1,0:T(4,128)(2,1)S(1)} %slice.40), channel_id=1, source_target_pairs={{0,1},{1,2},{2,3},{4,5},{5,6},{6,7},{8,9},{9,10},{10,11},{12,13},{... | collective-permute-start | bytes 294920 | tf_op jit(solution)/shard_map/ppermute | solution.py:20
  14.7 25.9 %copy-start.1 = (f32[256,256,1]{0,1,2:T(8,128)S(1)}, f32[256,256,1]{0,1,2:T(8,128)}, u32[]{:S(2)}) copy-start(f32[256,256,1]{0,1,2:T(8,128)} %constant.7) | copy-start | bytes 786436

commit v3 on v2

--- a/solution.py
+++ b/solution.py
@@ -89,7 +89,12 @@
 
     def send_from(g, spec, at):
         own_copy(g, spec, at).start()
-        each(1, n_inp, lambda d: turn_copy(g, d, spec, at).start())
+        first = n_inp // 2 - 1
+        each(
+            0,
+            n_inp - 1,
+            lambda k: turn_copy(g, 1 + lax.rem(k + first, n_inp - 1), spec, at).start(),
+        )
 
     def send(g):
         @pl.when(g < turn)

time: 393 us -> 387 us (0.985)
  Pallas kernels: 317 us -> 307 us
    pallas_call x1, Pallas kernels: 317 us -> 307 us  [per_device(): pl.pallas_call(functools.partial(exchange_and_correlate, n_inp, n_tm, ste...]
where the time goes in v3:
time: 387 us; the launch traced here: 383 us
  Pallas kernels  307 us (79%)
  local copies, waits for them, and re-layouts  31.6 us (8%)
  matrix products  23.6 us (6%)
  other arithmetic  15 us (4%)
    pallas_call x1, Pallas kernels, per_device(): pl.pallas_call(functools.partial(exchange_and_correlate, n_inp, n_tm, ste...  307 us
    dot_general x2, matrix products, per_device(): jnp.einsum('isn,nj->ijs', folded, jnp.asarray(table, jnp.float32), precis...  23.6 us
    convert_element_type x2, local copies, waits for them, and re-layouts, per_device(): side = jnp.einsum('isn,nj->ijs', folded, jnp.asarray(table, jnp.float32),...  15.6 us
    add x1, other arithmetic, filter_taps(): total + weights[tap][None, None, :] * extended[:, tap:tap + count, :].ast...  15 us
    unnamed x7, local copies, waits for them, and re-layouts  9.35 us
  transfers between devices with their start and end apart: 1, of which 1 were waited for; matrix products, arithmetic and copies ran while one was open for 0% of the time, Pallas kernels for 0%

profile of v3, /device:TPU:25, one launch (start us, length us, event | category | flops | bytes accessed | tf_op | source)
XLA Modules:
  0.0 382.7 jit_solution(3143837995247611782)
XLA Ops:
  0.0 0.0 copy-start.2
  0.0 9.3 %copy.8 = bf16[4,8,384,512]{3,2,1,0:T(8,128)(2,1)S(1)} copy(bf16[4,8,384,512]{3,1,2,0:T(8,128)(2,1)} %bitcast.26) | data formatting | bytes 25165824
  9.3 0.0 copy-start
  9.4 0.1 slice.40
  9.4 3.1 collective-permute-start
  12.6 0.0 copy-done.2
  12.6 2.1 collective-permute-done
  14.7 0.0 copy-start.1
  14.7 15.0 %multiply_add_fusion = f32[32,384,512]{2,1,0:T(8,128)} fusion(bf16[32,384,512]{2,1,0:T(8,128)(2,1)S(1)} %bitcast.22, bf16[32,3,512]{2,1,0:T(4,128)(2,1)S(1)} %collective-permute-done, f32[512]{0:T(512)S(1)} %bitcast.29, f32[512]{0:T(512)S(1)} %bitcast.30, f32[512]{0:T(512)S(1)} %bitcast.28, f32[512]{0:T(512)S(1)} %bitcast.27), kind=kLoop, calls=%fused_computation | loop fusion | flops 125829120 | bytes 37855232 | tf_op jit(solution)/shard_map/add | solution.py:26
  29.7 0.0 copy-done
  29.7 10.9 %convert_bitcast_fusion.1 = bf16[32,256,384]{2,1,0:T(8,128)(2,1)S(1)} fusion(f32[256,256,1]{0,1,2:T(8,128)S(1)} %copy-done, f32[32,384,512]{2,1,0:T(8,128)} %multiply_add_fusion), kind=kOutput, calls=%fused_computation.15 | convolution fusion | flops 4838129664 | bytes 31719424 | tf_op jit(solution)/shard_map/isn,nj->ijs/dot_general | solution.py:186
  40.6 0.0 copy-done.1
  40.7 12.7 %convert_bitcast_fusion = bf16[32,256,384]{2,1,0:T(8,128)(2,1)} fusion(f32[256,256,1]{0,1,2:T(8,128)S(1)} %copy-done.1, f32[32,384,512]{2,1,0:T(8,128)} %multiply_add_fusion), kind=kOutput, calls=%fused_computation.14 | convolution fusion | flops 4838129664 | bytes 31719424 | tf_op jit(solution)/shard_map/isn,nj->ijs/dot_general | solution.py:186
  53.3 9.1 %copy.6 = bf16[32,256,384]{2,0,1:T(8,128)(2,1)} copy(bf16[32,256,384]{2,1,0:T(8,128)(2,1)} %convert_bitcast_fusion) | data formatting | bytes 12582912 | tf_op jit(solution)/shard_map/convert_element_type | solution.py:192
  62.5 6.4 %copy.5 = bf16[32,256,384]{2,0,1:T(8,128)(2,1)} copy(bf16[32,256,384]{2,1,0:T(8,128)(2,1)S(1)} %convert_bitcast_fusion.1) | data formatting | bytes 12582912 | tf_op jit(solution)/shard_map/convert_element_type | solution.py:192
  68.9 307.1 %shard_map.46 = f32[32,2,64,256]{3,2,1,0:T(8,128)} custom-call(bf16[8,16,2,32,384]{4,3,2,1,0:T(8,128)(2,1)} %bitcast.24, bf16[8,16,2,32,384]{4,3,2,1,0:T(8,128)(2,1)} %bitcast.23), custom_call_target="tpu_custom_call" | custom-call | tf_op jit(solution)/shard_map/pallas_call | solution.py:199
  376.0 6.6 %copy.7 = f32[64,2,32,256]{3,2,1,0:T(8,128)} copy(f32[64,2,32,256]{3,0,1,2:T(8,128)} %bitcast.25) | data formatting | bytes 8388608 | tf_op jit(solution)/shard_map/transpose | solution.py:218
  (1 shorter events, 0.0 us)
Async XLA Ops:
  0.0 12.6 %copy-start.2 = (f32[4,512]{1,0:T(4,128)S(1)}, f32[4,512]{1,0:T(4,128)}, u32[]{:S(2)}) copy-start(f32[4,512]{1,0:T(4,128)} %param.5) | copy-start | bytes 24580
  9.3 20.4 %copy-start = (f32[256,256,1]{0,1,2:T(8,128)S(1)}, f32[256,256,1]{0,1,2:T(8,128)}, u32[]{:S(2)}) copy-start(f32[256,256,1]{0,1,2:T(8,128)} %constant.6) | copy-start | bytes 786436
  9.4 5.3 %collective-permute-start = (bf16[32,3,512]{2,1,0:T(4,128)(2,1)S(1)}, bf16[32,3,512]{2,1,0:T(4,128)(2,1)S(1)}, u32[]{:S(2)}, u32[]{:S(2)}) collective-permute-start(bf16[32,3,512]{2,1,0:T(4,128)(2,1)S(1)} %slice.40), channel_id=1, source_target_pairs={{0,1},{1,2},{2,3},{4,5},{5,6},{6,7},{8,9},{9,10},{10,11},{12,13},{... | collective-permute-start | bytes 294920 | tf_op jit(solution)/shard_map/ppermute | solution.py:20
  14.7 25.9 %copy-start.1 = (f32[256,256,1]{0,1,2:T(8,128)S(1)}, f32[256,256,1]{0,1,2:T(8,128)}, u32[]{:S(2)}) copy-start(f32[256,256,1]{0,1,2:T(8,128)} %constant.7) | copy-start | bytes 786436
